TPU v7x, 32 devices: a whole 2x2x4 slice. The times are simulated.
32 devices in a mesh: energy: 8 (over z, x), tile: 4 (over y, core).
Axes of the slice: x: 2, y: 2, z: 4, core: 2. Of those that a mesh axis runs over, the one named last changes fastest.
Arguments:
- object_tiles: float32 [8, 2, 4, 512, 512], P('energy', None, 'tile'), may hold values from -6 to 6
- probe_wave: float32 [8, 2, 256, 256], P('energy'), may hold values from -6 to 6
- measured: bfloat16 [8, 4, 16, 256, 256], P('energy', 'tile'), may hold values from 0 to 2
- positions: int32 [4, 16, 2], P('tile'), may hold values from 0 to 511, as said below
- materials: float32 [2, 8, 8], replicated, may hold values from -6 to 6
Outputs:
- fitted: float32 [8, 2, 4, 512, 512], P('energy', None, 'tile')
Inputs may be any that keep to these rules, and one draw needn't show every extreme that they name: `positions`: each entry is the corner of a 256 x 256 patch, given inside its tile; in every tile some patch has row corner 512 - 1 and some has column corner 512 - 1.
All inputs are finite; a program needn't handle non-finite values.
Results may differ from a plain program's by a relative error of at most 0.0013.
Values sent between devices are 32-bit elements; how exact they have to be, the bound alone decides.
A program may use at most 64 MiB of HBM per device.

v0:
```python
import math
import jax
import jax.numpy as jnp
from jax import lax
from jax.sharding import PartitionSpec as P

TILE_COLS = 4
FIT_STEPS = 10
amplitude_floor = 0.5


def shifted(value, axis, steps):
    count = lax.axis_size(axis)
    pairs = [(source, (source + steps) % count) for source in range(count)]
    return lax.ppermute(value, axis, pairs)


def fourier_tables(length, direction):
    counter = jnp.arange(length, dtype=jnp.int32)
    products = counter[:, None] * counter[None, :] % length
    angles = 2.0 * math.pi / length * products.astype(jnp.float32)
    cosine = jnp.cos(angles)
    sine = direction * jnp.sin(angles)
    left_table = jnp.concatenate(
        [jnp.concatenate([cosine, sine], 1), jnp.concatenate([-sine, cosine], 1)], 0
    ).astype(jnp.bfloat16)
    right_table = jnp.concatenate(
        [jnp.concatenate([cosine, -sine], 1), jnp.concatenate([sine, cosine], 1)], 0
    ).astype(jnp.bfloat16)
    return (left_table, right_table)


def transform(real_part, imag_part, left_table, right_table):
    length = real_part.shape[0]
    stacked = jnp.concatenate([real_part, imag_part], 0).astype(jnp.bfloat16)
    inner = jnp.dot(left_table, stacked, preferred_element_type=jnp.float32)
    beside = jnp.concatenate([inner[:length], inner[length:]], 1).astype(jnp.bfloat16)
    outer = jnp.dot(beside, right_table, preferred_element_type=jnp.float32) / length
    return (outer[:, :length], outer[:, length:])


def patch_gradient(
    field_real, field_imag, probe_real, probe_imag, amplitude, row_start, col_start, tables
):
    length = probe_real.shape[0]
    piece_real = lax.dynamic_slice(field_real, (row_start, col_start), (length, length))
    piece_imag = lax.dynamic_slice(field_imag, (row_start, col_start), (length, length))
    exit_real = probe_real * piece_real - probe_imag * piece_imag
    exit_imag = probe_real * piece_imag + probe_imag * piece_real
    far_real, far_imag = transform(exit_real, exit_imag, tables[0], tables[1])
    magnitude = jnp.sqrt(far_real * far_real + far_imag * far_imag)
    factor = amplitude.astype(jnp.float32) / jnp.maximum(magnitude, amplitude_floor) - 1.0
    back_real, back_imag = transform(factor * far_real, factor * far_imag, tables[2], tables[3])
    return (
        probe_real * back_real + probe_imag * back_imag,
        probe_real * back_imag - probe_imag * back_real,
    )


def fit_materials(data, materials):
    high = lax.Precision.HIGHEST
    gram = jnp.einsum("rem,ren->mn", materials, materials, precision=high)
    rate = 1.0 / jnp.trace(gram)
    target = jnp.einsum("rem,rep->mp", materials, data, precision=high)

    def descend(number, coefficients):
        slope = jnp.dot(gram, coefficients, precision=high) - target
        return jnp.maximum(coefficients - rate * slope, 0.0)

    return lax.fori_loop(0, FIT_STEPS, descend, jnp.zeros_like(target))


def fitted_spectra(materials, coefficients):
    return jnp.einsum("rem,mp->rep", materials, coefficients, precision=lax.Precision.HIGHEST)


def body(object_tiles, probe_wave, measured, positions, materials):
    own_object = object_tiles[0, :, 0]
    tile_px = own_object.shape[-1]
    length = probe_wave.shape[-1]
    count = measured.shape[2]
    tile_count = lax.axis_size("tile")
    row_step = TILE_COLS % tile_count
    right_strip = shifted(own_object[:, :, :length], "tile", -1)
    widened = jnp.concatenate([own_object, right_strip], 2)
    if row_step:
        lower_strip = shifted(widened[:, :length, :], "tile", -row_step)
    else:
        lower_strip = widened[:, :length, :]
    extended = jnp.concatenate([widened, lower_strip], 1)
    forward = fourier_tables(length, 1.0)
    inverse = fourier_tables(length, -1.0)
    tables = (forward[0], forward[1], inverse[0], inverse[1])
    probe_real = probe_wave[0, 0]
    probe_imag = probe_wave[0, 1]
    own_measured = measured[0, 0]
    corners = positions[0]
    anchor = jnp.zeros((), jnp.int32)

    def accumulate(number, gradient):
        row_start = corners[number, 0]
        col_start = corners[number, 1]
        term_real, term_imag = patch_gradient(
            extended[0],
            extended[1],
            probe_real,
            probe_imag,
            own_measured[number],
            row_start,
            col_start,
            tables,
        )
        current = lax.dynamic_slice(gradient, (anchor, row_start, col_start), (2, length, length))
        return lax.dynamic_update_slice(
            gradient, current + jnp.stack([term_real, term_imag]), (anchor, row_start, col_start)
        )

    gradient = lax.fori_loop(0, count, accumulate, jnp.zeros_like(extended))
    if row_step:
        from_above = shifted(gradient[:, tile_px:, :], "tile", row_step)
    else:
        from_above = gradient[:, tile_px:, :]
    upper = jnp.concatenate(
        [gradient[:, :length, :] + from_above, gradient[:, length:tile_px, :]], 1
    )
    from_left = shifted(upper[:, :, tile_px:], "tile", 1)
    summed = jnp.concatenate([upper[:, :, :length] + from_left, upper[:, :, length:tile_px]], 2)
    peak = jnp.max(probe_real * probe_real + probe_imag * probe_imag)
    updated = own_object + summed / peak
    groups = lax.axis_size("energy")
    pixels = tile_px * tile_px
    group_width = pixels // groups
    outgoing = updated.reshape(2, 1, groups, group_width)
    arrived = lax.all_to_all(outgoing, "energy", split_axis=2, concat_axis=1, tiled=True)
    coefficients = fit_materials(arrived.reshape(2, groups, group_width), materials)
    spectra = fitted_spectra(materials, coefficients).reshape(2, groups, 1, group_width)
    returned = lax.all_to_all(spectra, "energy", split_axis=1, concat_axis=2, tiled=True)
    result = returned.reshape(2, tile_px, tile_px)
    return result.reshape(1, 2, 1, tile_px, tile_px)


def solution(mesh):
    in_specs = (
        P("energy", None, "tile", None, None),
        P("energy", None, None, None),
        P("energy", "tile", None, None, None),
        P("tile", None, None),
        P(),
    )
    out_specs = P("energy", None, "tile", None, None)
    return jax.shard_map(body, mesh=mesh, in_specs=in_specs, out_specs=out_specs, check_vma=False)
```

profile of v0, /device:TPU:0, one launch (start us, length us, event | category | flops | bytes accessed | tf_op | source)
XLA Modules:
  0.0 486.9 jit_solution(13260882390065137983)
XLA Ops:
  8.8 8.5 %collective-permute-done = f32[2,512,256]{2,1,0:T(8,128)} collective-permute-done((f32[2,512,256]{2,1,0:T(8,128)}, f32[2,512,256]{2,1,0:T(8,128)}, u32[]{:S(2)}, u32[]{:S(2)}) %collective-permute-start) | collective-permute-done | bytes 1048608 | tf_op jit(solution)/shard_map/ppermute | solution.py:15
  23.7 303.1 %while.26 = (s32[]{:T(128)}, f32[2,768,768]{2,1,0:T(8,128)}, s32[16,2]{0,1:T(2,128)S(1)}, bf16[16,256,256]{2,1,0:T(8,128)(2,1)}, f32[2,768,768]{2,1,0:T(8,128)},...) while((s32[]{:T(128)}, f32[2,768,768]{2,1,0:T(8,128)}, ...), condition=%wide.region_1.2_spmd, body=%wide.region_0.1_spmd.sunk | while | flops 541392896 | bytes 21627124 | solution.py:118
  36.0 6.3 %dynamic_update_slice.11 = f32[2,768,768]{2,1,0:T(8,128)} dynamic-update-slice(f32[2,768,768]{2,1,0:T(8,128)} %get-tuple-element.519, f32[2,256,256]{2,1,0:T(8,128)S(1)} %maximum_add_fusion.2, s32[]{:T(128)} %constant.115.clone.1..sunk, s32[]{:T(128)S(6)} %select_n.102, s32[]{:T(128)S(6)} %select_n.103) | dynamic-update-slice | bytes 1048580 | tf_op jit(solution)/shard_map/while/body/eval_jaxpr/dynamic_update_slice | solution.py:114
  54.6 6.0 %dynamic_update_slice.11 = f32[2,768,768]{2,1,0:T(8,128)} dynamic-update-slice(f32[2,768,768]{2,1,0:T(8,128)} %get-tuple-element.519, f32[2,256,256]{2,1,0:T(8,128)S(1)} %maximum_add_fusion.2, s32[]{:T(128)} %constant.115.clone.1..sunk, s32[]{:T(128)S(6)} %select_n.102, s32[]{:T(128)S(6)} %select_n.103) | dynamic-update-slice | bytes 1048580 | tf_op jit(solution)/shard_map/while/body/eval_jaxpr/dynamic_update_slice | solution.py:114
  72.9 6.8 %dynamic_update_slice.11 = f32[2,768,768]{2,1,0:T(8,128)} dynamic-update-slice(f32[2,768,768]{2,1,0:T(8,128)} %get-tuple-element.519, f32[2,256,256]{2,1,0:T(8,128)S(1)} %maximum_add_fusion.2, s32[]{:T(128)} %constant.115.clone.1..sunk, s32[]{:T(128)S(6)} %select_n.102, s32[]{:T(128)S(6)} %select_n.103) | dynamic-update-slice | bytes 1048580 | tf_op jit(solution)/shard_map/while/body/eval_jaxpr/dynamic_update_slice | solution.py:114
  92.0 6.8 %dynamic_update_slice.11 = f32[2,768,768]{2,1,0:T(8,128)} dynamic-update-slice(f32[2,768,768]{2,1,0:T(8,128)} %get-tuple-element.519, f32[2,256,256]{2,1,0:T(8,128)S(1)} %maximum_add_fusion.2, s32[]{:T(128)} %constant.115.clone.1..sunk, s32[]{:T(128)S(6)} %select_n.102, s32[]{:T(128)S(6)} %select_n.103) | dynamic-update-slice | bytes 1048580 | tf_op jit(solution)/shard_map/while/body/eval_jaxpr/dynamic_update_slice | solution.py:114
  111.1 6.7 %dynamic_update_slice.11 = f32[2,768,768]{2,1,0:T(8,128)} dynamic-update-slice(f32[2,768,768]{2,1,0:T(8,128)} %get-tuple-element.519, f32[2,256,256]{2,1,0:T(8,128)S(1)} %maximum_add_fusion.2, s32[]{:T(128)} %constant.115.clone.1..sunk, s32[]{:T(128)S(6)} %select_n.102, s32[]{:T(128)S(6)} %select_n.103) | dynamic-update-slice | bytes 1048580 | tf_op jit(solution)/shard_map/while/body/eval_jaxpr/dynamic_update_slice | solution.py:114
  130.2 6.7 %dynamic_update_slice.11 = f32[2,768,768]{2,1,0:T(8,128)} dynamic-update-slice(f32[2,768,768]{2,1,0:T(8,128)} %get-tuple-element.519, f32[2,256,256]{2,1,0:T(8,128)S(1)} %maximum_add_fusion.2, s32[]{:T(128)} %constant.115.clone.1..sunk, s32[]{:T(128)S(6)} %select_n.102, s32[]{:T(128)S(6)} %select_n.103) | dynamic-update-slice | bytes 1048580 | tf_op jit(solution)/shard_map/while/body/eval_jaxpr/dynamic_update_slice | solution.py:114
  149.2 6.6 %dynamic_update_slice.11 = f32[2,768,768]{2,1,0:T(8,128)} dynamic-update-slice(f32[2,768,768]{2,1,0:T(8,128)} %get-tuple-element.519, f32[2,256,256]{2,1,0:T(8,128)S(1)} %maximum_add_fusion.2, s32[]{:T(128)} %constant.115.clone.1..sunk, s32[]{:T(128)S(6)} %select_n.102, s32[]{:T(128)S(6)} %select_n.103) | dynamic-update-slice | bytes 1048580 | tf_op jit(solution)/shard_map/while/body/eval_jaxpr/dynamic_update_slice | solution.py:114
  168.1 6.8 %dynamic_update_slice.11 = f32[2,768,768]{2,1,0:T(8,128)} dynamic-update-slice(f32[2,768,768]{2,1,0:T(8,128)} %get-tuple-element.519, f32[2,256,256]{2,1,0:T(8,128)S(1)} %maximum_add_fusion.2, s32[]{:T(128)} %constant.115.clone.1..sunk, s32[]{:T(128)S(6)} %select_n.102, s32[]{:T(128)S(6)} %select_n.103) | dynamic-update-slice | bytes 1048580 | tf_op jit(solution)/shard_map/while/body/eval_jaxpr/dynamic_update_slice | solution.py:114
  187.1 6.9 %dynamic_update_slice.11 = f32[2,768,768]{2,1,0:T(8,128)} dynamic-update-slice(f32[2,768,768]{2,1,0:T(8,128)} %get-tuple-element.519, f32[2,256,256]{2,1,0:T(8,128)S(1)} %maximum_add_fusion.2, s32[]{:T(128)} %constant.115.clone.1..sunk, s32[]{:T(128)S(6)} %select_n.102, s32[]{:T(128)S(6)} %select_n.103) | dynamic-update-slice | bytes 1048580 | tf_op jit(solution)/shard_map/while/body/eval_jaxpr/dynamic_update_slice | solution.py:114
  206.3 6.8 %dynamic_update_slice.11 = f32[2,768,768]{2,1,0:T(8,128)} dynamic-update-slice(f32[2,768,768]{2,1,0:T(8,128)} %get-tuple-element.519, f32[2,256,256]{2,1,0:T(8,128)S(1)} %maximum_add_fusion.2, s32[]{:T(128)} %constant.115.clone.1..sunk, s32[]{:T(128)S(6)} %select_n.102, s32[]{:T(128)S(6)} %select_n.103) | dynamic-update-slice | bytes 1048580 | tf_op jit(solution)/shard_map/while/body/eval_jaxpr/dynamic_update_slice | solution.py:114
  225.4 6.6 %dynamic_update_slice.11 = f32[2,768,768]{2,1,0:T(8,128)} dynamic-update-slice(f32[2,768,768]{2,1,0:T(8,128)} %get-tuple-element.519, f32[2,256,256]{2,1,0:T(8,128)S(1)} %maximum_add_fusion.2, s32[]{:T(128)} %constant.115.clone.1..sunk, s32[]{:T(128)S(6)} %select_n.102, s32[]{:T(128)S(6)} %select_n.103) | dynamic-update-slice | bytes 1048580 | tf_op jit(solution)/shard_map/while/body/eval_jaxpr/dynamic_update_slice | solution.py:114
  244.3 6.9 %dynamic_update_slice.11 = f32[2,768,768]{2,1,0:T(8,128)} dynamic-update-slice(f32[2,768,768]{2,1,0:T(8,128)} %get-tuple-element.519, f32[2,256,256]{2,1,0:T(8,128)S(1)} %maximum_add_fusion.2, s32[]{:T(128)} %constant.115.clone.1..sunk, s32[]{:T(128)S(6)} %select_n.102, s32[]{:T(128)S(6)} %select_n.103) | dynamic-update-slice | bytes 1048580 | tf_op jit(solution)/shard_map/while/body/eval_jaxpr/dynamic_update_slice | solution.py:114
  263.4 6.8 %dynamic_update_slice.11 = f32[2,768,768]{2,1,0:T(8,128)} dynamic-update-slice(f32[2,768,768]{2,1,0:T(8,128)} %get-tuple-element.519, f32[2,256,256]{2,1,0:T(8,128)S(1)} %maximum_add_fusion.2, s32[]{:T(128)} %constant.115.clone.1..sunk, s32[]{:T(128)S(6)} %select_n.102, s32[]{:T(128)S(6)} %select_n.103) | dynamic-update-slice | bytes 1048580 | tf_op jit(solution)/shard_map/while/body/eval_jaxpr/dynamic_update_slice | solution.py:114
  282.6 6.5 %dynamic_update_slice.11 = f32[2,768,768]{2,1,0:T(8,128)} dynamic-update-slice(f32[2,768,768]{2,1,0:T(8,128)} %get-tuple-element.519, f32[2,256,256]{2,1,0:T(8,128)S(1)} %maximum_add_fusion.2, s32[]{:T(128)} %constant.115.clone.1..sunk, s32[]{:T(128)S(6)} %select_n.102, s32[]{:T(128)S(6)} %select_n.103) | dynamic-update-slice | bytes 1048580 | tf_op jit(solution)/shard_map/while/body/eval_jaxpr/dynamic_update_slice | solution.py:114
  301.4 6.6 %dynamic_update_slice.11 = f32[2,768,768]{2,1,0:T(8,128)} dynamic-update-slice(f32[2,768,768]{2,1,0:T(8,128)} %get-tuple-element.519, f32[2,256,256]{2,1,0:T(8,128)S(1)} %maximum_add_fusion.2, s32[]{:T(128)} %constant.115.clone.1..sunk, s32[]{:T(128)S(6)} %select_n.102, s32[]{:T(128)S(6)} %select_n.103) | dynamic-update-slice | bytes 1048580 | tf_op jit(solution)/shard_map/while/body/eval_jaxpr/dynamic_update_slice | solution.py:114
  320.2 6.5 %dynamic_update_slice.11 = f32[2,768,768]{2,1,0:T(8,128)} dynamic-update-slice(f32[2,768,768]{2,1,0:T(8,128)} %get-tuple-element.519, f32[2,256,256]{2,1,0:T(8,128)S(1)} %maximum_add_fusion.2, s32[]{:T(128)} %constant.115.clone.1..sunk, s32[]{:T(128)S(6)} %select_n.102, s32[]{:T(128)S(6)} %select_n.103) | dynamic-update-slice | bytes 1048580 | tf_op jit(solution)/shard_map/while/body/eval_jaxpr/dynamic_update_slice | solution.py:114
  334.5 11.9 %collective-permute-done.1 = f32[2,512,256]{2,1,0:T(8,128)} collective-permute-done((f32[2,512,256]{2,1,0:T(8,128)}, f32[2,512,256]{2,1,0:T(8,128)}, u32[]{:S(2)}, u32[]{:S(2)}) %collective-permute-start.1) | collective-permute-done | bytes 1048608 | tf_op jit(solution)/shard_map/ppermute | solution.py:15
  358.2 5.8 %all-to-all-start = ((f32[2,1,8,32768]{3,0,1,2:T(2,128)}), f32[2,1,8,32768]{3,0,1,2:T(2,128)}, u32[]{:S(2)}, u32[]{:S(2)}) async-start(f32[2,1,8,32768]{3,0,1,2:T(2,128)} %copy.11), calls=%async_computation | async-start | bytes 4194304 | tf_op jit(solution)/shard_map/all_to_all | solution.py:134
  365.6 44.6 %all-to-all-done = f32[2,1,8,32768]{3,0,1,2:T(2,128)} async-done(((f32[2,1,8,32768]{3,0,1,2:T(2,128)}), f32[2,1,8,32768]{3,0,1,2:T(2,128)}, u32[]{:S(2)}, u32[]{:S(2)}) %all-to-all-start) | async-done | bytes 2097184 | tf_op jit(solution)/shard_map/all_to_all | solution.py:134
  410.2 3.9 convolution_bitcast_fusion.1
  414.1 12.5 %while.27 = (s32[]{:T(128)}, f32[8,32768]{1,0:T(8,128)S(1)}, f32[]{:T(128)}, f32[8,8]{1,0:T(8,128)S(1)}, f32[8,32768]{1,0:T(8,128)S(1)}, /*index=5*/s32[]{:T(128)}, s32[]{:T(128)}) while((s32[]{:T(128)}, f32[8,32768]{1,0:T(8,128)S(1)}, f32[]{:T(128)}, f32[8,8]{1,0:T(8,128)S(1)}, f32[8,32768]{1,0:T(8,128)S(1)}, ...), condition=%wide.region_5.6_spmd.clone, body=%wide.region_4.5_spmd.clone.sunk | while | flops 26738692 | bytes 5243227 | solution.py:70
  430.0 51.6 %all_to_all.8 = f32[2,8,1,32768]{3,0,2,1:T(2,128)S(1)} all-to-all(f32[2,8,1,32768]{3,0,2,1:T(2,128)S(1)} %copy.14), channel_id=1, replica_groups=mesh['energy'=8,'tile'=4] {'energy'}, dimensions={1} | all-to-all | bytes 4194304 | tf_op jit(solution)/shard_map/all_to_all | solution.py:137
  (249 shorter events, 191.4 us)
Async XLA Ops:
  0.0 364.1 %copy-start = (f32[2,8,8]{2,1,0:T(8,128)S(1)}, f32[2,8,8]{2,1,0:T(8,128)}, u32[]{:S(2)}) copy-start(f32[2,8,8]{2,1,0:T(8,128)} %param.13) | copy-start | bytes 1540
  2.3 6.5 %copy-start.4 = (f32[1,2,256,256]{3,2,1,0:T(8,128)S(1)}, f32[1,2,256,256]{3,2,1,0:T(8,128)}, u32[]{:S(2)}) copy-start(f32[1,2,256,256]{3,2,1,0:T(8,128)} %param.10) | copy-start | bytes 1572868
  2.3 15.1 %collective-permute-start = (f32[2,512,256]{2,1,0:T(8,128)}, f32[2,512,256]{2,1,0:T(8,128)}, u32[]{:S(2)}, u32[]{:S(2)}) collective-permute-start(f32[2,512,256]{2,1,0:T(8,128)} %slice.152), channel_id=1, source_target_pairs={{0,3},{1,0},{2,1},{3,2},{4,7},{5,4},{6,5},{7,6},{8,11},{9,8},{10,9... | collective-permute-start | bytes 3145736 | tf_op jit(solution)/shard_map/ppermute | solution.py:15
  6.7 10.6 %copy-start.3 = (f32[1,2,1,512,512]{4,3,2,1,0:T(8,128)S(1)}, f32[1,2,1,512,512]{4,3,2,1,0:T(8,128)}, u32[]{:S(2)}) copy-start(f32[1,2,1,512,512]{4,3,2,1,0:T(8,128)} %param.9) | copy-start | bytes 6291460
  21.2 2.5 copy-start.5
  329.4 1.5 copy-start.1
  330.9 15.4 %collective-permute-start.1 = (f32[2,512,256]{2,1,0:T(8,128)}, f32[2,512,256]{2,1,0:T(8,128)}, u32[]{:S(2)}, u32[]{:S(2)}) collective-permute-start(f32[2,512,256]{2,1,0:T(8,128)} %fusion.35), channel_id=1, source_target_pairs={{0,1},{1,2},{2,3},{3,0},{4,5},{5,6},{6,7},{7,4},{8,9},{9,10},{10,1... | collective-permute-start | bytes 3145736 | tf_op jit(solution)/shard_map/ppermute | solution.py:15
  334.5 13.5 %copy-start.2 = (f32[2,256,768]{2,1,0:T(8,128)S(1)}, f32[2,256,768]{2,1,0:T(8,128)}, u32[]{:S(2)}) copy-start(f32[2,256,768]{2,1,0:T(8,128)} %copy-done.1) | copy-start | bytes 4718596
  358.2 51.9 %all-to-all-start = ((f32[2,1,8,32768]{3,0,1,2:T(2,128)}), f32[2,1,8,32768]{3,0,1,2:T(2,128)}, u32[]{:S(2)}, u32[]{:S(2)}) async-start(f32[2,1,8,32768]{3,0,1,2:T(2,128)} %copy.11), calls=%async_computation | async-start | bytes 4194304 | tf_op jit(solution)/shard_map/all_to_all | solution.py:134
where the time goes:
time: 492 us; the launch traced here: 487 us
  local copies, waits for them, and re-layouts  181 us (37%)
  waiting for transfers between devices  65 us (13%)
  other arithmetic  62.6 us (13%)
  loops' own time  62.1 us (13%)
  matrix products  56 us (11%)
  blocking collectives  51.6 us (10%)
  starting transfers between devices  8.37 us (2%)
    dynamic_update_slice x16, local copies, waits for them, and re-layouts, accumulate(): lax.dynamic_update_slice(gradient, current + jnp.stack([term_real, term_i...  106 us
    another operation x1, loops' own time, body(): gradient = lax.fori_loop(0, count, accumulate, jnp.zeros_like(extended))  61.8 us
    all_to_all x1, blocking collectives, body(): lax.all_to_all(spectra, 'energy', split_axis=1, concat_axis=2, tiled=True)  51.6 us
    all_to_all x1, waiting for transfers between devices, body(): lax.all_to_all(outgoing, 'energy', split_axis=2, concat_axis=1, tiled=True)  44.6 us
    slice x16, local copies, waits for them, and re-layouts, accumulate(): extended[0]  42.9 us
    dot_general x32, matrix products, transform(): inner = jnp.dot(left_table, stacked, preferred_element_type=jnp.float32)  27.7 us
    another operation x35, other arithmetic  23.9 us
    add x16, other arithmetic, accumulate(): current + jnp.stack([term_real, term_imag])  22 us
  transfers between devices with their start and end apart: 3, of which 3 were waited for; matrix products, arithmetic and copies ran while one was open for 2% of the time, Pallas kernels for 0%

commit v1 on v0

--- a/solution.py
+++ b/solution.py
@@ -134,7 +134,9 @@
     arrived = lax.all_to_all(outgoing, "energy", split_axis=2, concat_axis=1, tiled=True)
     coefficients = fit_materials(arrived.reshape(2, groups, group_width), materials)
     spectra = fitted_spectra(materials, coefficients).reshape(2, groups, 1, group_width)
-    returned = lax.all_to_all(spectra, "energy", split_axis=1, concat_axis=2, tiled=True)
+    shards = jnp.split(spectra, lax.axis_size("energy"), axis=1)
+    got = lax.all_to_all(jnp.stack(shards), "energy", 0, 0)
+    returned = jnp.concatenate(got, axis=2)
     result = returned.reshape(2, tile_px, tile_px)
     return result.reshape(1, 2, 1, tile_px, tile_px)
 

time: 492 us -> 493 us (level)
  no operation moved by 1% of the time
where the time goes in v1:
time: 493 us; the launch traced here: 487 us
  local copies, waits for them, and re-layouts  181 us (37%)
  waiting for transfers between devices  65 us (13%)
  other arithmetic  62.6 us (13%)
  loops' own time  62.1 us (13%)
  matrix products  56 us (11%)
  blocking collectives  51.6 us (10%)
  starting transfers between devices  8.37 us (2%)
    dynamic_update_slice x16, local copies, waits for them, and re-layouts, accumulate(): lax.dynamic_update_slice(gradient, current + jnp.stack([term_real, term_i...  106 us
    another operation x1, loops' own time, body(): gradient = lax.fori_loop(0, count, accumulate, jnp.zeros_like(extended))  61.8 us
    all_to_all x1, blocking collectives, body(): got = lax.all_to_all(jnp.stack(shards), 'energy', 0, 0)  51.6 us
    all_to_all x1, waiting for transfers between devices, body(): lax.all_to_all(outgoing, 'energy', split_axis=2, concat_axis=1, tiled=True)  44.6 us
    slice x16, local copies, waits for them, and re-layouts, accumulate(): extended[0]  42.9 us
    dot_general x32, matrix products, transform(): inner = jnp.dot(left_table, stacked, preferred_element_type=jnp.float32)  27.7 us
    another operation x35, other arithmetic  23.9 us
    add x16, other arithmetic, accumulate(): current + jnp.stack([term_real, term_imag])  22 us
  transfers between devices with their start and end apart: 3, of which 3 were waited for; matrix products, arithmetic and copies ran while one was open for 2% of the time, Pallas kernels for 0%

profile of v1, /device:TPU:0, one launch (start us, length us, event | category | flops | bytes accessed | tf_op | source)
XLA Modules:
  0.0 487.1 jit_solution(17759296520986441641)
XLA Ops:
  8.8 8.5 %collective-permute-done = f32[2,512,256]{2,1,0:T(8,128)} collective-permute-done((f32[2,512,256]{2,1,0:T(8,128)}, f32[2,512,256]{2,1,0:T(8,128)}, u32[]{:S(2)}, u32[]{:S(2)}) %collective-permute-start) | collective-permute-done | bytes 1048608 | tf_op jit(solution)/shard_map/ppermute | solution.py:15
  23.7 303.1 %while.26 = (s32[]{:T(128)}, f32[2,768,768]{2,1,0:T(8,128)}, s32[16,2]{0,1:T(2,128)S(1)}, bf16[16,256,256]{2,1,0:T(8,128)(2,1)}, f32[2,768,768]{2,1,0:T(8,128)},...) while((s32[]{:T(128)}, f32[2,768,768]{2,1,0:T(8,128)}, ...), condition=%wide.region_1.2_spmd, body=%wide.region_0.1_spmd.sunk | while | flops 541392896 | bytes 21627124 | solution.py:118
  36.0 6.3 %dynamic_update_slice.11 = f32[2,768,768]{2,1,0:T(8,128)} dynamic-update-slice(f32[2,768,768]{2,1,0:T(8,128)} %get-tuple-element.519, f32[2,256,256]{2,1,0:T(8,128)S(1)} %maximum_add_fusion.2, s32[]{:T(128)} %constant.115.clone.1..sunk, s32[]{:T(128)S(6)} %select_n.102, s32[]{:T(128)S(6)} %select_n.103) | dynamic-update-slice | bytes 1048580 | tf_op jit(solution)/shard_map/while/body/eval_jaxpr/dynamic_update_slice | solution.py:114
  54.6 6.0 %dynamic_update_slice.11 = f32[2,768,768]{2,1,0:T(8,128)} dynamic-update-slice(f32[2,768,768]{2,1,0:T(8,128)} %get-tuple-element.519, f32[2,256,256]{2,1,0:T(8,128)S(1)} %maximum_add_fusion.2, s32[]{:T(128)} %constant.115.clone.1..sunk, s32[]{:T(128)S(6)} %select_n.102, s32[]{:T(128)S(6)} %select_n.103) | dynamic-update-slice | bytes 1048580 | tf_op jit(solution)/shard_map/while/body/eval_jaxpr/dynamic_update_slice | solution.py:114
  72.9 6.8 %dynamic_update_slice.11 = f32[2,768,768]{2,1,0:T(8,128)} dynamic-update-slice(f32[2,768,768]{2,1,0:T(8,128)} %get-tuple-element.519, f32[2,256,256]{2,1,0:T(8,128)S(1)} %maximum_add_fusion.2, s32[]{:T(128)} %constant.115.clone.1..sunk, s32[]{:T(128)S(6)} %select_n.102, s32[]{:T(128)S(6)} %select_n.103) | dynamic-update-slice | bytes 1048580 | tf_op jit(solution)/shard_map/while/body/eval_jaxpr/dynamic_update_slice | solution.py:114
  92.0 6.8 %dynamic_update_slice.11 = f32[2,768,768]{2,1,0:T(8,128)} dynamic-update-slice(f32[2,768,768]{2,1,0:T(8,128)} %get-tuple-element.519, f32[2,256,256]{2,1,0:T(8,128)S(1)} %maximum_add_fusion.2, s32[]{:T(128)} %constant.115.clone.1..sunk, s32[]{:T(128)S(6)} %select_n.102, s32[]{:T(128)S(6)} %select_n.103) | dynamic-update-slice | bytes 1048580 | tf_op jit(solution)/shard_map/while/body/eval_jaxpr/dynamic_update_slice | solution.py:114
  111.1 6.7 %dynamic_update_slice.11 = f32[2,768,768]{2,1,0:T(8,128)} dynamic-update-slice(f32[2,768,768]{2,1,0:T(8,128)} %get-tuple-element.519, f32[2,256,256]{2,1,0:T(8,128)S(1)} %maximum_add_fusion.2, s32[]{:T(128)} %constant.115.clone.1..sunk, s32[]{:T(128)S(6)} %select_n.102, s32[]{:T(128)S(6)} %select_n.103) | dynamic-update-slice | bytes 1048580 | tf_op jit(solution)/shard_map/while/body/eval_jaxpr/dynamic_update_slice | solution.py:114
  130.2 6.7 %dynamic_update_slice.11 = f32[2,768,768]{2,1,0:T(8,128)} dynamic-update-slice(f32[2,768,768]{2,1,0:T(8,128)} %get-tuple-element.519, f32[2,256,256]{2,1,0:T(8,128)S(1)} %maximum_add_fusion.2, s32[]{:T(128)} %constant.115.clone.1..sunk, s32[]{:T(128)S(6)} %select_n.102, s32[]{:T(128)S(6)} %select_n.103) | dynamic-update-slice | bytes 1048580 | tf_op jit(solution)/shard_map/while/body/eval_jaxpr/dynamic_update_slice | solution.py:114
  149.2 6.6 %dynamic_update_slice.11 = f32[2,768,768]{2,1,0:T(8,128)} dynamic-update-slice(f32[2,768,768]{2,1,0:T(8,128)} %get-tuple-element.519, f32[2,256,256]{2,1,0:T(8,128)S(1)} %maximum_add_fusion.2, s32[]{:T(128)} %constant.115.clone.1..sunk, s32[]{:T(128)S(6)} %select_n.102, s32[]{:T(128)S(6)} %select_n.103) | dynamic-update-slice | bytes 1048580 | tf_op jit(solution)/shard_map/while/body/eval_jaxpr/dynamic_update_slice | solution.py:114
  168.1 6.8 %dynamic_update_slice.11 = f32[2,768,768]{2,1,0:T(8,128)} dynamic-update-slice(f32[2,768,768]{2,1,0:T(8,128)} %get-tuple-element.519, f32[2,256,256]{2,1,0:T(8,128)S(1)} %maximum_add_fusion.2, s32[]{:T(128)} %constant.115.clone.1..sunk, s32[]{:T(128)S(6)} %select_n.102, s32[]{:T(128)S(6)} %select_n.103) | dynamic-update-slice | bytes 1048580 | tf_op jit(solution)/shard_map/while/body/eval_jaxpr/dynamic_update_slice | solution.py:114
  187.1 6.9 %dynamic_update_slice.11 = f32[2,768,768]{2,1,0:T(8,128)} dynamic-update-slice(f32[2,768,768]{2,1,0:T(8,128)} %get-tuple-element.519, f32[2,256,256]{2,1,0:T(8,128)S(1)} %maximum_add_fusion.2, s32[]{:T(128)} %constant.115.clone.1..sunk, s32[]{:T(128)S(6)} %select_n.102, s32[]{:T(128)S(6)} %select_n.103) | dynamic-update-slice | bytes 1048580 | tf_op jit(solution)/shard_map/while/body/eval_jaxpr/dynamic_update_slice | solution.py:114
  206.3 6.8 %dynamic_update_slice.11 = f32[2,768,768]{2,1,0:T(8,128)} dynamic-update-slice(f32[2,768,768]{2,1,0:T(8,128)} %get-tuple-element.519, f32[2,256,256]{2,1,0:T(8,128)S(1)} %maximum_add_fusion.2, s32[]{:T(128)} %constant.115.clone.1..sunk, s32[]{:T(128)S(6)} %select_n.102, s32[]{:T(128)S(6)} %select_n.103) | dynamic-update-slice | bytes 1048580 | tf_op jit(solution)/shard_map/while/body/eval_jaxpr/dynamic_update_slice | solution.py:114
  225.4 6.6 %dynamic_update_slice.11 = f32[2,768,768]{2,1,0:T(8,128)} dynamic-update-slice(f32[2,768,768]{2,1,0:T(8,128)} %get-tuple-element.519, f32[2,256,256]{2,1,0:T(8,128)S(1)} %maximum_add_fusion.2, s32[]{:T(128)} %constant.115.clone.1..sunk, s32[]{:T(128)S(6)} %select_n.102, s32[]{:T(128)S(6)} %select_n.103) | dynamic-update-slice | bytes 1048580 | tf_op jit(solution)/shard_map/while/body/eval_jaxpr/dynamic_update_slice | solution.py:114
  244.3 6.9 %dynamic_update_slice.11 = f32[2,768,768]{2,1,0:T(8,128)} dynamic-update-slice(f32[2,768,768]{2,1,0:T(8,128)} %get-tuple-element.519, f32[2,256,256]{2,1,0:T(8,128)S(1)} %maximum_add_fusion.2, s32[]{:T(128)} %constant.115.clone.1..sunk, s32[]{:T(128)S(6)} %select_n.102, s32[]{:T(128)S(6)} %select_n.103) | dynamic-update-slice | bytes 1048580 | tf_op jit(solution)/shard_map/while/body/eval_jaxpr/dynamic_update_slice | solution.py:114
  263.4 6.8 %dynamic_update_slice.11 = f32[2,768,768]{2,1,0:T(8,128)} dynamic-update-slice(f32[2,768,768]{2,1,0:T(8,128)} %get-tuple-element.519, f32[2,256,256]{2,1,0:T(8,128)S(1)} %maximum_add_fusion.2, s32[]{:T(128)} %constant.115.clone.1..sunk, s32[]{:T(128)S(6)} %select_n.102, s32[]{:T(128)S(6)} %select_n.103) | dynamic-update-slice | bytes 1048580 | tf_op jit(solution)/shard_map/while/body/eval_jaxpr/dynamic_update_slice | solution.py:114
  282.6 6.5 %dynamic_update_slice.11 = f32[2,768,768]{2,1,0:T(8,128)} dynamic-update-slice(f32[2,768,768]{2,1,0:T(8,128)} %get-tuple-element.519, f32[2,256,256]{2,1,0:T(8,128)S(1)} %maximum_add_fusion.2, s32[]{:T(128)} %constant.115.clone.1..sunk, s32[]{:T(128)S(6)} %select_n.102, s32[]{:T(128)S(6)} %select_n.103) | dynamic-update-slice | bytes 1048580 | tf_op jit(solution)/shard_map/while/body/eval_jaxpr/dynamic_update_slice | solution.py:114
  301.4 6.6 %dynamic_update_slice.11 = f32[2,768,768]{2,1,0:T(8,128)} dynamic-update-slice(f32[2,768,768]{2,1,0:T(8,128)} %get-tuple-element.519, f32[2,256,256]{2,1,0:T(8,128)S(1)} %maximum_add_fusion.2, s32[]{:T(128)} %constant.115.clone.1..sunk, s32[]{:T(128)S(6)} %select_n.102, s32[]{:T(128)S(6)} %select_n.103) | dynamic-update-slice | bytes 1048580 | tf_op jit(solution)/shard_map/while/body/eval_jaxpr/dynamic_update_slice | solution.py:114
  320.2 6.5 %dynamic_update_slice.11 = f32[2,768,768]{2,1,0:T(8,128)} dynamic-update-slice(f32[2,768,768]{2,1,0:T(8,128)} %get-tuple-element.519, f32[2,256,256]{2,1,0:T(8,128)S(1)} %maximum_add_fusion.2, s32[]{:T(128)} %constant.115.clone.1..sunk, s32[]{:T(128)S(6)} %select_n.102, s32[]{:T(128)S(6)} %select_n.103) | dynamic-update-slice | bytes 1048580 | tf_op jit(solution)/shard_map/while/body/eval_jaxpr/dynamic_update_slice | solution.py:114
  334.5 11.9 %collective-permute-done.1 = f32[2,512,256]{2,1,0:T(8,128)} collective-permute-done((f32[2,512,256]{2,1,0:T(8,128)}, f32[2,512,256]{2,1,0:T(8,128)}, u32[]{:S(2)}, u32[]{:S(2)}) %collective-permute-start.1) | collective-permute-done | bytes 1048608 | tf_op jit(solution)/shard_map/ppermute | solution.py:15
  358.2 5.8 %all-to-all-start = ((f32[2,1,8,32768]{3,0,1,2:T(2,128)}), f32[2,1,8,32768]{3,0,1,2:T(2,128)}, u32[]{:S(2)}, u32[]{:S(2)}) async-start(f32[2,1,8,32768]{3,0,1,2:T(2,128)} %copy.37), calls=%async_computation | async-start | bytes 4194304 | tf_op jit(solution)/shard_map/all_to_all | solution.py:134
  365.6 44.6 %all-to-all-done = f32[2,1,8,32768]{3,0,1,2:T(2,128)} async-done(((f32[2,1,8,32768]{3,0,1,2:T(2,128)}), f32[2,1,8,32768]{3,0,1,2:T(2,128)}, u32[]{:S(2)}, u32[]{:S(2)}) %all-to-all-start) | async-done | bytes 2097184 | tf_op jit(solution)/shard_map/all_to_all | solution.py:134
  410.2 3.9 convolution_bitcast_fusion
  414.1 12.5 %while.27 = (s32[]{:T(128)}, f32[8,32768]{1,0:T(8,128)S(1)}, f32[]{:T(128)}, f32[8,8]{1,0:T(8,128)S(1)}, f32[8,32768]{1,0:T(8,128)S(1)}, /*index=5*/s32[]{:T(128)}, s32[]{:T(128)}) while((s32[]{:T(128)}, f32[8,32768]{1,0:T(8,128)S(1)}, f32[]{:T(128)}, f32[8,8]{1,0:T(8,128)S(1)}, f32[8,32768]{1,0:T(8,128)S(1)}, ...), condition=%wide.region_5.6_spmd.clone, body=%wide.region_4.5_spmd.clone.sunk | while | flops 26738692 | bytes 5243227 | solution.py:70
  430.3 51.6 %all_to_all.14 = f32[8,2,1,1,32768]{4,2,3,1,0:T(1,128)S(1)} all-to-all(f32[8,2,1,1,32768]{4,2,3,1,0:T(1,128)S(1)} %fusion.47), channel_id=1, replica_groups=mesh['energy'=8,'tile'=4] {'energy'}, dimensions={0} | all-to-all | bytes 4194304 | tf_op jit(solution)/shard_map/all_to_all | solution.py:138
  (256 shorter events, 191.6 us)
Async XLA Ops:
  0.0 364.1 %copy-start = (f32[2,8,8]{2,1,0:T(8,128)S(1)}, f32[2,8,8]{2,1,0:T(8,128)}, u32[]{:S(2)}) copy-start(f32[2,8,8]{2,1,0:T(8,128)} %param.13) | copy-start | bytes 1540
  2.3 6.5 %copy-start.4 = (f32[1,2,256,256]{3,2,1,0:T(8,128)S(1)}, f32[1,2,256,256]{3,2,1,0:T(8,128)}, u32[]{:S(2)}) copy-start(f32[1,2,256,256]{3,2,1,0:T(8,128)} %param.10) | copy-start | bytes 1572868
  2.3 15.1 %collective-permute-start = (f32[2,512,256]{2,1,0:T(8,128)}, f32[2,512,256]{2,1,0:T(8,128)}, u32[]{:S(2)}, u32[]{:S(2)}) collective-permute-start(f32[2,512,256]{2,1,0:T(8,128)} %slice.152), channel_id=1, source_target_pairs={{0,3},{1,0},{2,1},{3,2},{4,7},{5,4},{6,5},{7,6},{8,11},{9,8},{10,9... | collective-permute-start | bytes 3145736 | tf_op jit(solution)/shard_map/ppermute | solution.py:15
  6.7 10.6 %copy-start.3 = (f32[1,2,1,512,512]{4,3,2,1,0:T(8,128)S(1)}, f32[1,2,1,512,512]{4,3,2,1,0:T(8,128)}, u32[]{:S(2)}) copy-start(f32[1,2,1,512,512]{4,3,2,1,0:T(8,128)} %param.9) | copy-start | bytes 6291460
  21.2 2.5 copy-start.5
  329.4 1.5 copy-start.1
  330.9 15.4 %collective-permute-start.1 = (f32[2,512,256]{2,1,0:T(8,128)}, f32[2,512,256]{2,1,0:T(8,128)}, u32[]{:S(2)}, u32[]{:S(2)}) collective-permute-start(f32[2,512,256]{2,1,0:T(8,128)} %fusion.35), channel_id=1, source_target_pairs={{0,1},{1,2},{2,3},{3,0},{4,5},{5,6},{6,7},{7,4},{8,9},{9,10},{10,1... | collective-permute-start | bytes 3145736 | tf_op jit(solution)/shard_map/ppermute | solution.py:15
  334.5 13.5 %copy-start.2 = (f32[2,256,768]{2,1,0:T(8,128)S(1)}, f32[2,256,768]{2,1,0:T(8,128)}, u32[]{:S(2)}) copy-start(f32[2,256,768]{2,1,0:T(8,128)} %copy-done.1) | copy-start | bytes 4718596
  358.2 51.9 %all-to-all-start = ((f32[2,1,8,32768]{3,0,1,2:T(2,128)}), f32[2,1,8,32768]{3,0,1,2:T(2,128)}, u32[]{:S(2)}, u32[]{:S(2)}) async-start(f32[2,1,8,32768]{3,0,1,2:T(2,128)} %copy.37), calls=%async_computation | async-start | bytes 4194304 | tf_op jit(solution)/shard_map/all_to_all | solution.py:134
